TPU v7x, 256 devices: a whole 4x4x8 slice. The times are simulated.
256 devices in a mesh: rows: 64 (over z, x, core), grp: 4 (over y).
Axes of the slice: x: 4, y: 4, z: 8, core: 2. Of those that a mesh axis runs over, the one named last changes fastest.
Arguments:
- observations: float32 [524288, 512], P(('rows', 'grp')), may hold values from -32 to 32, as said below
- sensor_ids: int32 [524288], P(('rows', 'grp')), may hold values from 0 to 127
- sensor_sigma: float32 [128], replicated, may hold values from 0.3 to 3
- buckets: int32 [524288], P(('rows', 'grp')), may hold values from 0 to 63, as said below
- prior_factor: float32 [512, 512], replicated, may hold values from -0.3 to 3, as said below
Outputs:
- whitened: float32 [524288, 512], P(('rows', 'grp'))
- info_factor: float32 [512, 512], replicated
Inputs may be any that keep to these rules, and one draw needn't show every extreme that they name: `buckets`: in each aligned block of 2048 rows every bucket index appears exactly 32 times. `observations`: rows are real-valued without further structure. `prior_factor`: upper triangular with a positive diagonal of at least 0.5.
All inputs are finite; a program needn't handle non-finite values.
Results may differ from a plain program's by a relative error of at most 0.00007.
Values sent between devices are 32-bit elements; how exact they have to be, the bound alone decides.
A program may use at most 128 MiB of HBM per device.

v0:
```python
import jax
import jax.numpy as jnp
from jax import lax
from jax.sharding import PartitionSpec as P


def matmul(left, right):
    return jnp.dot(left, right, precision=lax.Precision.HIGHEST, preferred_element_type=jnp.float32)


def outer_sum(values):
    return lax.dot_general(
        values,
        values,
        (((0,), (0,)), ((), ())),
        precision=lax.Precision.HIGHEST,
        preferred_element_type=jnp.float32,
    )


def square_form(matrix):
    return matmul(matrix.T, matrix)


def lower_inverse(lower):
    width = lower.shape[0]
    identity = jnp.eye(width, dtype=jnp.float32)
    diag_values = jnp.diagonal(lower)
    scaled_lower = lower / diag_values[:, None]
    nilpotent = identity - scaled_lower
    product = identity + nilpotent
    power = nilpotent
    reach = 2
    while reach < width:
        power = matmul(power, power)
        product = product + matmul(product, power)
        reach = reach * 2
    return product / diag_values[None, :]


def upper_factor(matrix):
    return jnp.linalg.cholesky(matrix).T


def whiten_rows(values, factor):
    inverse = lower_inverse(factor.T)
    return matmul(values, inverse.T)


def regroup_rows(values, target):
    outgoing = jnp.zeros_like(values).at[target].set(values)
    return lax.all_to_all(outgoing, "rows", split_axis=0, concat_axis=0, tiled=True)


def reduce_gram(local_gram, prior_gram, total_rows):
    summed = lax.psum(local_gram, ("rows", "grp"))
    return upper_factor(prior_gram + summed / jnp.float32(total_rows))


def shards(observations, sensor_ids, sensor_sigma, buckets, prior_factor):
    rows_dev = observations.shape[0]
    row_groups = lax.axis_size("rows")
    devices = lax.axis_size(("rows", "grp"))
    per_bucket = rows_dev // row_groups
    total_rows = rows_dev * devices
    inv_sigma = 1.0 / sensor_sigma
    matches = sensor_ids[:, None] == jnp.arange(sensor_sigma.shape[0], dtype=jnp.int32)[None, :]
    row_scale = jnp.sum(jnp.where(matches, inv_sigma[None, :], jnp.float32(0.0)), axis=1)
    scaled = observations * row_scale[:, None]
    onehot = (buckets[:, None] == jnp.arange(row_groups, dtype=jnp.int32)[None, :]).astype(
        jnp.int32
    )
    running = jnp.cumsum(onehot, axis=0)
    within = jnp.sum(onehot * running, axis=1) - 1
    target = buckets * per_bucket + within
    prior_gram = square_form(prior_factor)
    received = regroup_rows(scaled, target)
    factor = reduce_gram(outer_sum(received), prior_gram, total_rows)
    whitened = whiten_rows(received, factor)
    return (whitened, factor)


def solution(mesh):
    in_specs = (P(("rows", "grp"), None), P(("rows", "grp")), P(), P(("rows", "grp")), P())
    out_specs = (P(("rows", "grp"), None), P())
    return jax.shard_map(shards, mesh=mesh, in_specs=in_specs, out_specs=out_specs, check_vma=False)
```

profile of v0, /device:TPU:1, one launch (start us, length us, event | category | flops | bytes accessed | tf_op | source)
XLA Modules:
  0.0 559.4 jit_solution(9048692939131870598)
XLA Ops:
  7.2 0.0 copy-start
  7.2 0.0 copy-start.5
  7.2 0.0 all-reduce.3.cloned.1.call-start
  7.2 0.7 broadcast_divide_fusion
  8.0 0.7 fusion.8
  8.7 18.1 %reduce-window.6 = s32[64,16,128]{2,1,0:T(8,128)S(1)} reduce-window(s32[64,16,128]{2,1,0:T(8,128)S(1)} %fusion.8, s32[]{:T(128)} %constant.151.clone.1), window={size=1x1x128 pad=0_0x0_0x127_0}, to_apply=%region_0.1 | reduce-window | flops 16646144 | bytes 1048580 | tf_op jit(solution)/shard_map/reduce-window
  26.9 0.2 slice.91
  27.1 0.4 copy.35
  27.5 0.2 reduce-window.9
  27.7 0.2 broadcast_add_fusion
  27.9 0.2 fusion.7
  28.1 0.6 select_reduce_fusion
  28.8 13.0 %scatter_custom_fusion = f32[2048,512]{1,0:T(8,128)} fusion(s32[2048]{0:T(1024)S(1)} %compare_select_fusion, f32[2048,512]{1,0:T(8,128)} %param.5, f32[2048]{0:T(1024)S(1)} %select_reduce_fusion, f32[]{:T(128)} %constant.149.clone.1), kind=kCustom, calls=%fused_computation.2 | custom fusion | flops 1048576 | bytes 8396804 | tf_op jit(solution)/shard_map/scatter | solution.py:51
  41.7 107.6 %all_to_all.12 = f32[64,32,512]{2,1,0:T(8,128)S(1)} all-to-all(f32[64,32,512]{2,1,0:T(8,128)} %bitcast.84), channel_id=1, replica_groups=mesh['rows'=64,'grp'=4] {'rows'}, dimensions={0} | all-to-all | bytes 8388608 | tf_op jit(solution)/shard_map/all_to_all | solution.py:52
  149.3 2.0 copy-done.1
  151.3 8.0 %convolution_bitcast_fusion = f32[512,512]{0,1:T(8,128)} fusion(f32[64,32,512]{2,1,0:T(8,128)S(1)} %all_to_all.12), kind=kOutput, calls=%fused_computation.17 | convolution fusion | flops 6442450944 | bytes 5242880 | tf_op jit(solution)/shard_map/dot_general | solution.py:12
  159.4 0.0 all-reduce.3.cloned.1.call-update
  159.4 252.4 %all-reduce.3.cloned.1.call-done = f32[512,512]{0,1:T(8,128)} async-done(((f32[512,512]{0,1:T(8,128)}), f32[512,512]{0,1:T(8,128)}) %all-reduce.3.cloned.1.call-update) | async-done | bytes 1048592 | tf_op jit(solution)/shard_map/psum | solution.py:56
  411.8 0.0 copy-done
  411.8 3.1 convolution_add_fusion.8
  414.9 0.3 copy.31
  415.3 0.2 fusion.5
  415.5 0.0 copy-start.3
  415.5 1.0 copy-done.3
  416.5 12.2 %cholesky.104 = f32[128,128]{1,0:T(8,128)S(1)} custom-call(f32[128,128]{1,0:T(8,128)S(1)} %cholesky.266), custom_call_target="Cholesky" | custom-call | tf_op jit(solution)/shard_map/jit(cholesky)/cholesky | solution.py:42
  428.7 0.1 cholesky.224
  428.9 9.8 %custom-call.27 = f32[1,128,128]{1,2,0:T(8,128)S(1)} custom-call(f32[1,128,128]{2,1,0:T(8,128)S(1)} %get-tuple-element.19), custom_call_target="InvertDiagBlocksLowerTriangular" | custom-call | tf_op jit(solution)/shard_map/jit(cholesky)/cholesky | solution.py:42
  438.7 1.2 constant_dynamic-update-slice_fusion.2
  439.9 1.3 convolution_subtract_fusion
  441.2 11.7 %cholesky.217 = f32[128,128]{1,0:T(8,128)S(1)} custom-call(f32[128,128]{1,0:T(8,128)S(1)} %cholesky.270), custom_call_target="Cholesky" | custom-call | tf_op jit(solution)/shard_map/jit(cholesky)/cholesky | solution.py:42
  452.9 9.8 %custom-call.28 = f32[1,128,128]{1,2,0:T(8,128)S(1)} custom-call(f32[1,128,128]{2,1,0:T(8,128)S(1)} %get-tuple-element.16), custom_call_target="InvertDiagBlocksLowerTriangular" | custom-call | tf_op jit(solution)/shard_map/jit(cholesky)/cholesky | solution.py:42
  462.8 0.3 convolution_dynamic-update-slice_fusion
  463.0 1.3 convolution_subtract_fusion.1
  464.3 11.9 %cholesky.238 = f32[128,128]{1,0:T(8,128)S(1)} custom-call(f32[128,128]{1,0:T(8,128)S(1)} %cholesky.275), custom_call_target="Cholesky" | custom-call | tf_op jit(solution)/shard_map/jit(cholesky)/cholesky | solution.py:42
  476.2 0.7 compare_reduce_fusion.1
  477.0 9.8 %custom-call.29 = f32[1,128,128]{1,2,0:T(8,128)S(1)} custom-call(f32[1,128,128]{2,1,0:T(8,128)S(1)} %get-tuple-element.13), custom_call_target="InvertDiagBlocksLowerTriangular" | custom-call | tf_op jit(solution)/shard_map/jit(cholesky)/cholesky | solution.py:42
  486.8 0.2 convolution_dynamic-update-slice_fusion.1
  487.0 1.2 convolution_subtract_fusion.2
  488.2 11.7 %cholesky.255 = f32[128,128]{1,0:T(8,128)S(1)} custom-call(f32[128,128]{1,0:T(8,128)S(1)} %convolution_subtract_fusion.2), custom_call_target="Cholesky" | custom-call | tf_op jit(solution)/shard_map/jit(cholesky)/cholesky | solution.py:42
  500.0 0.6 compare_reduce_fusion
  500.6 0.7 compare_reduce_fusion.2
  503.8 0.1 select_select_fusion
  503.9 1.2 fusion.65
  505.1 4.7 gather_fusion
  509.8 2.1 fusion.20
  512.0 3.0 convolution_add_fusion.7
  514.9 1.8 fusion.21
  516.8 2.5 copy.32
  519.3 1.8 fusion.22
  521.2 0.0 copy-done.4
  521.2 1.8 convolution_add_fusion.6
  523.0 1.8 fusion.23
  524.9 1.8 convolution_add_fusion.5
  526.7 2.3 fusion.24
  529.0 1.9 convolution_add_fusion.4
  530.9 1.8 fusion.25
  532.7 1.8 convolution_add_fusion.3
  534.6 1.8 fusion.26
  536.4 1.9 convolution_add_fusion.2
  538.3 1.8 fusion.27
  540.1 0.0 copy-start.2
  540.1 2.0 convolution_add_fusion.1
  542.2 1.9 fusion.4
  544.1 8.3 %fusion.28 = f32[2048,512]{1,0:T(8,128)} fusion(f32[2048,512]{1,0:T(8,128)S(1)} %bitcast.82, f32[512,512]{1,0:T(8,128)S(1)} %fusion.4), kind=kOutput, calls=%fused_computation.77 | convolution fusion | flops 6442450944 | bytes 9437184 | tf_op jit(solution)/shard_map/dot_general | solution.py:8
  (15 shorter events, 0.2 us)
Async XLA Ops:
  7.2 404.7 %copy-start = (f32[512,512]{1,0:T(8,128)S(1)}, f32[512,512]{1,0:T(8,128)}, u32[]{:S(2)}) copy-start(f32[512,512]{1,0:T(8,128)} %param.9) | copy-start | bytes 3145732
  7.2 20.7 %copy-start.5 = (s32[2048]{0:T(1024)S(1)}, s32[2048]{0:T(1024)}, u32[]{:S(2)}) copy-start(s32[2048]{0:T(1024)} %param.8) | copy-start | bytes 24580
  7.2 20.9 %copy-start.6 = (s32[2048]{0:T(1024)S(1)}, s32[2048]{0:T(1024)}, u32[]{:S(2)}) copy-start(s32[2048]{0:T(1024)} %param.6) | copy-start | bytes 24580
  7.2 404.6 %all-reduce.3.cloned.1.call-start = ((), (), s32[]{:S(2)}) async-start(), calls=%async_computation.1 | async-start | bytes 2097152 | tf_op jit(solution)/shard_map/psum | solution.py:56
  149.3 2.0 copy-start.1
  415.5 1.0 copy-start.3
  514.9 6.2 %copy-start.4 = (f32[512,512]{1,0:T(8,128)S(1)}, f32[512,512]{1,0:T(8,128)}, u32[]{:S(2)}) copy-start(f32[512,512]{1,0:T(8,128)} %convolution_add_fusion.7) | copy-start | bytes 3145732
  540.1 3.9 copy-start.2
Sparse Core Ops, SparseCore 0:
  159.5 252.2 all-reduce.2
where the time goes:
time: 565 us; the launch traced here: 559 us
  waiting for transfers between devices  252 us (45%)
  other arithmetic  114 us (20%)
  blocking collectives  108 us (19%)
  matrix products  56.4 us (10%)
  between operations  17.1 us (3%)
  local copies, waits for them, and re-layouts  11.4 us (2%)
    psum x1, waiting for transfers between devices, reduce_gram(): summed = lax.psum(local_gram, ('rows', 'grp'))  252 us
    all_to_all x1, blocking collectives, regroup_rows(): lax.all_to_all(outgoing, 'rows', split_axis=0, concat_axis=0, tiled=True)  108 us
    another operation x14, other arithmetic, upper_factor(): return jnp.linalg.cholesky(matrix).T  79.1 us
    dot_general x18, matrix products, matmul(): jnp.dot(left, right, precision=lax.Precision.HIGHEST, preferred_element_t...  42.9 us
    another operation x3, other arithmetic  18.5 us
    scatter x1, other arithmetic, regroup_rows(): outgoing = jnp.zeros_like(values).at[target].set(values)  13 us
  transfers between devices with their start and end apart: 1, of which 1 were waited for; matrix products, arithmetic and copies ran while one was open for 0% of the time, Pallas kernels for 0%

commit v1 on v0

v1 whole, which is shorter than its diff:
```python
import functools

import jax
import jax.numpy as jnp
from jax import lax
from jax.experimental import pallas as pl
from jax.experimental.pallas import tpu as pltpu
from jax.sharding import PartitionSpec as P

MESH = pl.DeviceIdType.MESH
F32, BF16, I32 = jnp.float32, jnp.bfloat16, jnp.int32
NZ, NX, NC, NY = 8, 4, 2, 4
STEPS = (4, 1, 7, 3, 5, 2, 6, 0)
PANEL = 128


def iota(shape, dim):
    return lax.broadcasted_iota(I32, shape, dim)


def split(values):
    high = values.astype(BF16)
    return high, (values - high.astype(F32)).astype(BF16)


def dot(left, right, dims=((1,), (0,))):
    return lax.dot_general(left, right, (dims, ((), ())), preferred_element_type=F32)


def exact_dot(left, right, dims=((1,), (0,))):
    return lax.dot_general(
        left, right, (dims, ((), ())), precision=lax.Precision.HIGHEST, preferred_element_type=F32
    )


def factor_panel(block):
    tiles = PANEL // 8
    lane = iota((8, PANEL), 1)
    sub = iota((8, PANEL), 0)
    rows = [block[8 * q : 8 * q + 8] for q in range(tiles)]
    invs = [jnp.where(lane == sub + 8 * q, jnp.float32(1.0), jnp.float32(0.0)) for q in range(tiles)]
    for j in range(PANEL):
        p, k = j // 8, j % 8
        pivot_row = rows[p][k : k + 1]
        inv_row = invs[p][k : k + 1]
        root = lax.rsqrt(pivot_row[:, j : j + 1])
        unit_row, unit_inv = pivot_row * root, inv_row * root
        for q in range(p, tiles):
            column = rows[q][:, j : j + 1] * root
            if q == p:
                below = sub > k
                here = sub == k
                new_rows = rows[q] - column * unit_row
                new_invs = invs[q] - column * unit_inv
                rows[q] = jnp.where(below, new_rows, jnp.where(here, unit_row, rows[q]))
                invs[q] = jnp.where(below, new_invs, jnp.where(here, unit_inv, invs[q]))
            else:
                rows[q] = rows[q] - column * unit_row
                invs[q] = invs[q] - column * unit_inv
    return jnp.concatenate(rows, axis=0), jnp.concatenate(invs, axis=0)


def kernel(
    total_rows,
    x_hbm, ids_ref, sigma_ref, buckets_ref, prior_ref,
    out_ref, factor_ref,
    x_buf, high_ref, low_ref, pick_ref, target_ref, scale_ref, sorted_ref, recv_ref,
    gram_ref, pair_ref, half_ref, plane_ref, tiles_ref, line_ref, gather_ref, info_ref, inv_ref, prior_gram_ref,
    inv_high_ref, inv_low_ref,
    x_sem, send_sem, recv_sem, pair_sem, plane_sem, line_sem, line_back_sem, plane_back_sem, pair_back_sem,
):
    me, y = lax.axis_index("rows"), lax.axis_index("grp")
    z, x, c = me // (NX * NC), (me // NC) % NX, me % NC
    rows_dev, state = x_hbm.shape
    groups, per_group = NX * NC, NZ
    block = rows_dev // (NZ * NX * NC)
    chunk = block * per_group

    def row_index(dz, dx, dc):
        return (((z + dz) % NZ) * NX + (x + dx) % NX) * NC + (c + dc) % NC

    loads = []
    for g in range(groups):
        part = pl.ds(g * chunk, chunk)
        copy = pltpu.make_async_copy(x_hbm.at[part], x_buf.at[part], x_sem.at[g])
        copy.start()
        loads.append(copy)

    barrier = pltpu.get_barrier_semaphore()
    for dz in range(NZ):
        for dx in range(NX):
            for dc in range(NC):
                if (dz, dx, dc) != (0, 0, 0):
                    pl.semaphore_signal(
                        barrier, inc=1, device_id={"rows": row_index(dz, dx, dc)}, device_id_type=MESH
                    )
    for dx in range(NX):
        for dy in range(1, NY):
            peer = {"rows": row_index(0, dx, 0), "grp": (y + dy) % NY}
            pl.semaphore_signal(barrier, inc=1, device_id=peer, device_id_type=MESH)

    n_buckets, n_chunks = NZ * NX * NC, rows_dev // 128
    below = (iota((128, 256), 0) <= iota((128, 256), 1)) | (iota((128, 256), 1) >= 128)
    counter = jnp.where(below, jnp.float32(1.0), jnp.float32(0.0)).astype(BF16)
    bucket_no = iota((n_buckets, 128), 0)
    base = jnp.zeros((n_buckets, 128), F32)
    for q in range(n_chunks):
        match = bucket_no == buckets_ref[q : q + 1, :]
        onehot = jnp.where(match, jnp.float32(1.0), jnp.float32(0.0))
        counts = dot(onehot.astype(BF16), counter)
        rank = counts[:, :128] + base
        base = base + counts[:, 128:]
        spot = jnp.where(match, rank.astype(I32) + (bucket_no * block - 1), 0)
        target_ref[:, 128 * q : 128 * q + 128] = jnp.broadcast_to(
            jnp.sum(spot, axis=0, keepdims=True), (8, 128)
        )

    weights = jnp.broadcast_to(1.0 / sigma_ref[...], (128, 128)).T
    w_high, w_mid = split(weights)
    w_low = (weights - w_high.astype(F32) - w_mid.astype(F32)).astype(BF16)
    sensor_no = iota((128, 128), 0)
    for q in range(n_chunks):
        onehot = jnp.where(sensor_no == ids_ref[q : q + 1, :], jnp.float32(1.0), jnp.float32(0.0)).T.astype(BF16)
        scale_ref[128 * q : 128 * q + 128, :] = (
            dot(onehot, w_high) + dot(onehot, w_mid) + dot(onehot, w_low)
        )

    @pl.loop(0, groups)
    def _(g):
        part = pl.ds(pl.multiple_of(g * chunk, chunk), chunk)
        pltpu.make_async_copy(x_hbm.at[part], x_buf.at[part], x_sem.at[g]).wait()
        scale = scale_ref[part, :]
        for n in range(state // 128):
            cols = slice(128 * n, 128 * n + 128)
            high, low = split(x_buf[part, cols] * scale)
            high_ref[part, cols] = high
            low_ref[part, cols] = low

    pl.semaphore_wait(barrier, NZ * NX * NC - 1 + NX * (NY - 1))

    def offsets(g, j):
        return STEPS[j], (g // NC + j) % NX, g % NC

    def is_own(g, j):
        dz, dx, dc = offsets(g, j)
        return (dz == 0) & (dx == 0) & (dc == 0)

    def row_copy(g, j):
        spot = pl.ds(pl.multiple_of(g * chunk + j * block, block), block)
        return pltpu.make_async_remote_copy(
            sorted_ref.at[spot], recv_ref.at[spot],
            send_sem.at[g * per_group + j], recv_sem.at[g * per_group + j],
            device_id={"rows": row_index(*offsets(g, j))}, device_id_type=MESH,
        )

    def sort_and_send(g):
        for j in range(per_group):
            first = row_index(*offsets(g, j)) * block
            for i in range(block // 8):
                hit = target_ref[...] == iota((8, rows_dev), 0) + (first + 8 * i)
                pick_ref[j * block + 8 * i : j * block + 8 * i + 8, :] = jnp.where(
                    hit, jnp.float32(1.0), jnp.float32(0.0)
                ).astype(BF16)
        part = pl.ds(pl.multiple_of(g * chunk, chunk), chunk)
        pick = pick_ref[...]
        sorted_ref[part, :] = dot(pick, high_ref[...]) + dot(pick, low_ref[...])
        for j in range(per_group):
            if STEPS[j] == 0:
                own = is_own(g, j)
                spot = pl.ds(pl.multiple_of(g * chunk + j * block, block), block)

                @pl.when(own)
                def _():
                    recv_ref[spot, :] = sorted_ref[spot, :]

                @pl.when(jnp.logical_not(own))
                def _():
                    row_copy(g, j).start()
            else:
                row_copy(g, j).start()

    def sort_groups(first, last):
        @pl.loop(first, last)
        def _(g):
            sort_and_send(g)

    sort_groups(0, 1)

    gram_ref[...] = jnp.zeros_like(gram_ref)

    @pl.loop(0, groups)
    def _(g):
        part = pl.ds(pl.multiple_of(g * chunk, chunk), chunk)
        high, low = high_ref[part, :], low_ref[part, :]
        along = ((0,), (0,))
        gram_ref[...] += dot(high, high, along) + dot(high, low, along) + dot(low, high, along)

    half_rows = state // NC
    piece_rows = half_rows // (NX * NY)
    mine_half = pl.ds(pl.multiple_of(c * half_rows, half_rows), half_rows)
    other_half = pl.ds(pl.multiple_of((1 - c) * half_rows, half_rows), half_rows)
    partner = {"rows": row_index(0, 0, 1)}
    pair = pltpu.make_async_remote_copy(
        gram_ref.at[other_half], pair_ref, pair_sem.at[0], pair_sem.at[1], device_id=partner, device_id_type=MESH
    )
    pair.start()

    prior = prior_ref[...]
    prior_gram_ref[...] = exact_dot(prior, prior, ((0,), (0,)))
    sort_groups(1, 2)
    pair.wait_recv()
    half_ref[...] = gram_ref[mine_half, :] + pair_ref[...]

    def piece(px, py):
        return pl.ds(pl.multiple_of((px * NY + py) * piece_rows, piece_rows), piece_rows)

    plane = [(dx, dy) for dx in range(NX) for dy in range(NY) if (dx, dy) != (0, 0)]
    plane_copies = []
    for n, (dx, dy) in enumerate(plane):
        px, py = (x + dx) % NX, (y + dy) % NY
        copy = pltpu.make_async_remote_copy(
            half_ref.at[piece(px, py)], plane_ref.at[n], plane_sem.at[0, n], plane_sem.at[1, n],
            device_id={"rows": row_index(0, dx, 0), "grp": py}, device_id_type=MESH,
        )
        copy.start()
        plane_copies.append(copy)
    sort_groups(2, 4)
    for copy in plane_copies:
        copy.wait_recv()
    total = half_ref[piece(x, y), :]
    for n in range(len(plane)):
        total = total + plane_ref[n]
    for t in range(NZ):
        tiles_ref[t] = total[8 * (t // 4) : 8 * (t // 4) + 8, 128 * (t % 4) : 128 * (t % 4) + 128]
    line_copies = []
    for dz in range(1, NZ):
        copy = pltpu.make_async_remote_copy(
            tiles_ref.at[(z + dz) % NZ], line_ref.at[dz], line_sem.at[0, dz], line_sem.at[1, dz],
            device_id={"rows": row_index(dz, 0, 0)}, device_id_type=MESH,
        )
        copy.start()
        line_copies.append(copy)
    sort_groups(4, 6)
    for copy in line_copies:
        copy.wait_recv()
    done = tiles_ref[z]
    for dz in range(1, NZ):
        done = done + line_ref[dz]
    gather_ref[z] = done
    back_copies = []
    for dz in range(1, NZ):
        copy = pltpu.make_async_remote_copy(
            gather_ref.at[z], gather_ref.at[z], line_back_sem.at[0, dz], line_back_sem.at[1, dz],
            device_id={"rows": row_index(dz, 0, 0)}, device_id_type=MESH,
        )
        copy.start()
        back_copies.append(copy)
    sort_groups(6, 8)
    for copy in back_copies:
        copy.wait_recv()
    own_piece = pl.ds(
        pl.multiple_of(c * half_rows + (x * NY + y) * piece_rows, piece_rows), piece_rows
    )
    info_ref[own_piece, :] = jnp.concatenate(
        [jnp.concatenate([gather_ref[4 * a + b] for b in range(4)], axis=1) for a in range(2)], axis=0
    )
    plane_back = []
    for n, (dx, dy) in enumerate(plane):
        copy = pltpu.make_async_remote_copy(
            info_ref.at[own_piece], info_ref.at[own_piece], plane_back_sem.at[0, n], plane_back_sem.at[1, n],
            device_id={"rows": row_index(0, dx, 0), "grp": (y + dy) % NY}, device_id_type=MESH,
        )
        copy.start()
        plane_back.append(copy)
    for copy in plane_back:
        copy.wait_recv()
    pair_back = pltpu.make_async_remote_copy(
        info_ref.at[mine_half], info_ref.at[mine_half], pair_back_sem.at[0], pair_back_sem.at[1],
        device_id=partner, device_id_type=MESH,
    )
    pair_back.start()
    for copies in ([pair], plane_copies, line_copies, back_copies, plane_back):
        for copy in copies:
            copy.wait_send()
    pair_back.wait()

    gram_ref[...] = prior_gram_ref[...] + info_ref[...] / jnp.float32(total_rows)
    inv_ref[...] = jnp.where(iota((state, state), 0) == iota((state, state), 1), jnp.float32(1.0), jnp.float32(0.0))

    @pl.loop(0, state // PANEL)
    def _(k):
        part = pl.ds(pl.multiple_of(k * PANEL, PANEL), PANEL)
        upper, inverse = factor_panel(gram_ref[part, part])
        del upper
        wide = exact_dot(inverse, gram_ref[part, :])
        wide_inv = exact_dot(inverse, inv_ref[part, :])
        row_no = k * PANEL + iota((PANEL, state), 0)
        col_no = iota((PANEL, state), 1)
        wide = jnp.where(col_no >= row_no, wide, jnp.float32(0.0))
        factor_ref[part, :] = wide
        inv_ref[part, :] = wide_inv
        rest = jnp.where(col_no >= (k + 1) * PANEL, wide, jnp.float32(0.0))
        gram_ref[...] = gram_ref[...] - exact_dot(rest, wide, ((0,), (0,)))
        inv_ref[...] = inv_ref[...] - exact_dot(rest, wide_inv, ((0,), (0,)))

    inv_high_ref[...], inv_low_ref[...] = split(inv_ref[...])

    @pl.loop(0, groups)
    def _(g):
        for j in range(per_group):
            if STEPS[j] == 0:
                @pl.when(jnp.logical_not(is_own(g, j)))
                def _():
                    row_copy(g, j).wait()
            else:
                row_copy(g, j).wait()
        part = pl.ds(pl.multiple_of(g * chunk, chunk), chunk)
        high, low = split(recv_ref[part, :])
        inv_high, inv_low = inv_high_ref[...], inv_low_ref[...]
        cross = ((1,), (1,))
        white = dot(high, inv_high, cross) + dot(high, inv_low, cross) + dot(low, inv_high, cross)
        for j in range(per_group):
            dz, dx, dc = offsets(g, j)
            source = row_index(NZ - dz, NX - dx, NC - dc)
            spot = pl.ds(pl.multiple_of(source * block, block), block)
            out_ref[spot, :] = white[j * block : (j + 1) * block]


def shards(observations, sensor_ids, sensor_sigma, buckets, prior_factor):
    rows_dev, state = observations.shape
    total_rows = rows_dev * lax.axis_size(("rows", "grp"))
    vmem = pl.BlockSpec(memory_space=pltpu.VMEM)
    half = state // NC
    piece = half // (NX * NY)
    dma = pltpu.SemaphoreType.DMA
    return pl.pallas_call(
        functools.partial(kernel, total_rows),
        out_shape=(
            jax.ShapeDtypeStruct((rows_dev, state), F32),
            jax.ShapeDtypeStruct((state, state), F32),
        ),
        in_specs=[pl.BlockSpec(memory_space=pl.ANY), vmem, vmem, vmem, vmem],
        out_specs=(vmem, vmem),
        scratch_shapes=[
            pltpu.VMEM((rows_dev, state), F32),
            pltpu.VMEM((rows_dev, state), BF16),
            pltpu.VMEM((rows_dev, state), BF16),
            pltpu.VMEM((rows_dev // (NX * NC), rows_dev), BF16),
            pltpu.VMEM((8, rows_dev), I32),
            pltpu.VMEM((rows_dev, 128), F32),
            pltpu.VMEM((rows_dev, state), F32),
            pltpu.VMEM((rows_dev, state), F32),
            pltpu.VMEM((state, state), F32),
            pltpu.VMEM((half, state), F32),
            pltpu.VMEM((half, state), F32),
            pltpu.VMEM((NX * NY - 1, piece, state), F32),
            pltpu.VMEM((NZ, 8, 128), F32),
            pltpu.VMEM((NZ, 8, 128), F32),
            pltpu.VMEM((NZ, 8, 128), F32),
            pltpu.VMEM((state, state), F32),
            pltpu.VMEM((state, state), F32),
            pltpu.VMEM((state, state), F32),
            pltpu.VMEM((state, state), BF16),
            pltpu.VMEM((state, state), BF16),
            dma((NX * NC,)),
            dma((NZ * NX * NC,)),
            dma((NZ * NX * NC,)),
            dma((2,)),
            dma((2, NX * NY - 1)),
            dma((2, NZ)),
            dma((2, NZ)),
            dma((2, NX * NY - 1)),
            dma((2,)),
        ],
        compiler_params=pltpu.CompilerParams(
            collective_id=0, has_side_effects=True, vmem_limit_bytes=48 << 20
        ),
    )(
        observations,
        sensor_ids.reshape(-1, 128),
        sensor_sigma.reshape(1, -1),
        buckets.reshape(-1, 128),
        prior_factor,
    )


def solution(mesh):
    in_specs = (P(("rows", "grp"), None), P(("rows", "grp")), P(), P(("rows", "grp")), P())
    out_specs = (P(("rows", "grp"), None), P())
    return jax.shard_map(shards, mesh=mesh, in_specs=in_specs, out_specs=out_specs, check_vma=False)
```

time: 565 us -> 171 us (0.30)
  waiting for transfers between devices: 252 us -> 0 us
  Pallas kernels: 0 us -> 161 us
  other arithmetic: 114 us -> 0 us
  blocking collectives: 108 us -> 0 us
  matrix products: 56.4 us -> 0 us
  between operations: 17.1 us -> 0.65 us
    psum x1 -> x0, waiting for transfers between devices: 252 us -> none  [reduce_gram(): summed = lax.psum(local_gram, ('rows', 'grp'))]
    pallas_call x0 -> x1, Pallas kernels: none -> 161 us  [shards(): pl.pallas_call(functools.partial(kernel, total_rows), out_shape=(jax.Shap...]
    all_to_all x1 -> x0, blocking collectives: 108 us -> none  [regroup_rows(): lax.all_to_all(outgoing, 'rows', split_axis=0, concat_axis=0, tiled=True)]
    another operation x17 -> x0, other arithmetic: 97.6 us -> none  [the longest x14 79.1 us: upper_factor(): return jnp.linalg.cholesky(matrix).T]
    dot_general x19 -> x0, matrix products: 51 us -> none  [the longest x18 42.9 us: matmul(): jnp.dot(left, right, precision=lax.Precision.HIGHEST, preferred_element_t...]
    scatter x1 -> x0, other arithmetic: 13 us -> none  [regroup_rows(): outgoing = jnp.zeros_like(values).at[target].set(values)]
  transfers between devices with their start and end apart: 1 -> 0, of which waited for: 1 -> 0; matrix products, arithmetic and copies ran while one was open for 0% -> 0% of each run, Pallas kernels for 0% -> 0%
where the time goes in v1:
time: 171 us; the launch traced here: 170 us
  Pallas kernels  161 us (94%)
  local copies, waits for them, and re-layouts  8.88 us (5%)
    pallas_call x1, Pallas kernels, shards(): pl.pallas_call(functools.partial(kernel, total_rows), out_shape=(jax.Shap...  161 us
    unnamed x10, local copies, waits for them, and re-layouts  8.88 us

profile of v1, /device:TPU:1, one launch (start us, length us, event | category | flops | bytes accessed | tf_op | source)
XLA Modules:
  0.0 170.4 jit_solution(8751176790374654424)
XLA Ops:
  0.6 0.0 copy-start
  0.6 1.2 copy-done
  1.9 0.0 copy-start.1
  1.9 0.7 copy-done.1
  2.6 0.0 copy-start.2
  2.6 0.7 copy-done.2
  3.3 0.0 copy-start.3
  3.3 0.7 copy-done.3
  3.9 160.9 %shard_map.68 = (f32[2048,512]{1,0:T(8,128)}, f32[512,512]{1,0:T(8,128)S(1)}) custom-call(f32[2048,512]{1,0:T(8,128)} %x_hbm.1, s32[16,128]{1,0:T(8,128)S(1)} %bitcast.3, f32[1,128]{1,0:T(1,128)S(1)} %bitcast.5, s32[16,128]{1,0:T(8,128)S(1)} %bitcast.4, f32[512,512]{1,0:T(8,128)S(1)} %copy-done), custom_call_target="tpu_custom_call" | custom-call | tf_op jit(solution)/shard_map/pallas_call | solution.py:336
  164.8 4.6 %copy.9 = f32[2048,512]{1,0:T(8,128)} copy(f32[2048,512]{1,0:T(8,128)} %get-tuple-element.4) | data formatting | bytes 8388608
  169.4 1.0 copy.10
Async XLA Ops:
  0.6 1.2 copy-start
  1.9 0.7 copy-start.1
  2.6 0.7 copy-start.2
  3.3 0.7 copy-start.3

commit v2 on v1

--- a/solution.py
+++ b/solution.py
@@ -33,41 +33,109 @@
     )
 
 
-def factor_panel(block):
+def along(piece):
+    return jnp.broadcast_to(piece, (8, PANEL))
+
+
+def root_of(value):
+    root = lax.rsqrt(value)
+    return root, root * root
+
+
+def inverse_panel(block):
     tiles = PANEL // 8
-    lane = iota((8, PANEL), 1)
-    sub = iota((8, PANEL), 0)
+    lane, sub = iota((8, PANEL), 1), iota((8, PANEL), 0)
+    zero = jnp.float32(0.0)
     rows = [block[8 * q : 8 * q + 8] for q in range(tiles)]
-    invs = [jnp.where(lane == sub + 8 * q, jnp.float32(1.0), jnp.float32(0.0)) for q in range(tiles)]
-    for j in range(PANEL):
-        p, k = j // 8, j % 8
-        pivot_row = rows[p][k : k + 1]
-        inv_row = invs[p][k : k + 1]
-        root = lax.rsqrt(pivot_row[:, j : j + 1])
-        unit_row, unit_inv = pivot_row * root, inv_row * root
-        for q in range(p, tiles):
-            column = rows[q][:, j : j + 1] * root
-            if q == p:
-                below = sub > k
-                here = sub == k
-                new_rows = rows[q] - column * unit_row
-                new_invs = invs[q] - column * unit_inv
-                rows[q] = jnp.where(below, new_rows, jnp.where(here, unit_row, rows[q]))
-                invs[q] = jnp.where(below, new_invs, jnp.where(here, unit_inv, invs[q]))
-            else:
-                rows[q] = rows[q] - column * unit_row
-                invs[q] = invs[q] - column * unit_inv
-    return jnp.concatenate(rows, axis=0), jnp.concatenate(invs, axis=0)
+    invs = [jnp.where(lane == sub + 8 * q, jnp.float32(1.0), zero) for q in range(tiles)]
+    outs = []
+    for p in range(tiles):
+        scale = jnp.zeros((8, PANEL), F32)
+        for k in (0, 4):
+            cols = {
+                q: [along(rows[q][:, 8 * p + k + n : 8 * p + k + n + 1]) for n in range(4)] for q in range(p, tiles)
+            }
+            m = [[along(cols[p][n][k + i : k + i + 1]) for n in range(4)] for i in range(4)]
+            a, b, d = m[0][0], m[1][0], m[1][1]
+            det = a * d - b * b
+            root_a, inv_a = root_of(a)
+            root_det, inv_det = root_of(det)
+            b02, b03, b12, b13 = m[2][0], m[3][0], m[2][1], m[3][1]
+            g02, g12 = (d * b02 - b * b12) * inv_det, (a * b12 - b * b02) * inv_det
+            g03, g13 = (d * b03 - b * b13) * inv_det, (a * b13 - b * b03) * inv_det
+            s22 = m[2][2] - b02 * g02 - b12 * g12
+            s32 = m[3][2] - b03 * g02 - b13 * g12
+            s33 = m[3][3] - b03 * g03 - b13 * g13
+            low_det = s22 * s33 - s32 * s32
+            root_s, inv_s = root_of(s22)
+            root_low, inv_low = root_of(low_det)
+            f, h = b * inv_a, s32 * inv_s
+            for i, root in enumerate((root_a, root_det * (a * root_a), root_s, root_low * (s22 * root_s))):
+                scale = jnp.where(sub == k + i, root, scale)
+
+            def eliminate(t0, t1, t2, t3):
+                t2 = t2 - g02 * t0 - g12 * t1
+                t3 = t3 - g03 * t0 - g13 * t1
+                return t0, t1 - f * t0, t2, t3 - h * t2
+
+            weights = (inv_a, a * inv_det, inv_s, s22 * inv_low)
+            pivot_rows = eliminate(*(along(rows[p][k + i : k + i + 1]) for i in range(4)))
+            pivot_invs = eliminate(*(along(invs[p][k + i : k + i + 1]) for i in range(4)))
+            pivot_rows = [value * w for value, w in zip(pivot_rows, weights)]
+            pivot_invs = [value * w for value, w in zip(pivot_invs, weights)]
+            for q in range(p, tiles):
+                x = eliminate(*cols[q])
+                if q == p:
+                    x = [jnp.where(sub > k + i, x[i], zero) for i in range(4)]
+                for held, pivots in ((rows, pivot_rows), (invs, pivot_invs)):
+                    held[q] = held[q] - (
+                        (x[0] * pivots[0] + x[1] * pivots[1]) + (x[2] * pivots[2] + x[3] * pivots[3])
+                    )
+        outs.append(invs[p] * scale)
+    return jnp.concatenate(outs, axis=0)
+
+
+def factor_and_invert(matrix_ref, factor_ref, inv_ref):
+    state = matrix_ref.shape[0]
+    panels = state // PANEL
+    factor_ref[...] = jnp.zeros_like(factor_ref)
+    down = ((0,), (0,))
+
+    @pl.loop(0, panels)
+    def _(k):
+        part = pl.ds(pl.multiple_of(k * PANEL, PANEL), PANEL)
+        inverse = inverse_panel(matrix_ref[part, part])
+        for s in range(panels):
+
+            @pl.when(k == s)
+            def _():
+                first, last = s * PANEL, (s + 1) * PANEL
+                own = slice(first, last)
+                wide = exact_dot(inverse, matrix_ref[own, first:])
+                keep = iota((PANEL, PANEL), 1) >= iota((PANEL, PANEL), 0)
+                factor_ref[own, own] = jnp.where(keep, wide[:, :PANEL], jnp.float32(0.0))
+                inv_ref[own, own] = inverse
+                if s:
+                    inv_ref[own, :first] = exact_dot(inverse, inv_ref[own, :first])
+                if s < panels - 1:
+                    rest = wide[:, PANEL:]
+                    factor_ref[own, last:] = rest
+                    inv_ref[own, last:] = jnp.zeros((PANEL, state - last), F32)
+                    matrix_ref[last:, last:] = matrix_ref[last:, last:] - exact_dot(rest, rest, down)
+                    delta = exact_dot(rest, inv_ref[own, :last], down)
+                    if s:
+                        inv_ref[last:, :first] = inv_ref[last:, :first] - delta[:, :first]
+                    inv_ref[last:, own] = -delta[:, first:]
 
 
 def kernel(
     total_rows,
-    x_hbm, ids_ref, sigma_ref, buckets_ref, prior_ref,
+    x_hbm, ids_hbm, sigma_hbm, buckets_hbm, prior_hbm,
     out_ref, factor_ref,
-    x_buf, high_ref, low_ref, pick_ref, target_ref, scale_ref, sorted_ref, recv_ref,
+    ids_ref, sigma_ref, buckets_ref, prior_ref, x_buf, high_ref, low_ref, pick_ref, target_ref, scale_ref, sorted_ref, recv_ref,
     gram_ref, pair_ref, half_ref, plane_ref, tiles_ref, line_ref, gather_ref, info_ref, inv_ref, prior_gram_ref,
     inv_high_ref, inv_low_ref,
-    x_sem, send_sem, recv_sem, pair_sem, plane_sem, line_sem, line_back_sem, plane_back_sem, pair_back_sem,
+    small_sem, x_sem, send_sem, recv_sem, pair_sem, plane_sem, line_sem, line_back_sem, plane_back_sem, pair_back_sem,
 ):
     me, y = lax.axis_index("rows"), lax.axis_index("grp")
     z, x, c = me // (NX * NC), (me // NC) % NX, me % NC
@@ -79,12 +147,19 @@
     def row_index(dz, dx, dc):
         return (((z + dz) % NZ) * NX + (x + dx) % NX) * NC + (c + dc) % NC
 
-    loads = []
+    smalls = [
+        pltpu.make_async_copy(source, target, small_sem.at[n])
+        for n, (source, target) in enumerate(
+            ((buckets_hbm, buckets_ref), (ids_hbm, ids_ref), (sigma_hbm, sigma_ref), (prior_hbm, prior_ref))
+        )
+    ]
+    for copy in smalls[:3]:
+        copy.start()
     for g in range(groups):
         part = pl.ds(g * chunk, chunk)
         copy = pltpu.make_async_copy(x_hbm.at[part], x_buf.at[part], x_sem.at[g])
         copy.start()
-        loads.append(copy)
+    smalls[3].start()
 
     barrier = pltpu.get_barrier_semaphore()
     for dz in range(NZ):
@@ -98,6 +173,8 @@
         for dy in range(1, NY):
             peer = {"rows": row_index(0, dx, 0), "grp": (y + dy) % NY}
             pl.semaphore_signal(barrier, inc=1, device_id=peer, device_id_type=MESH)
+
+    smalls[0].wait()
 
     n_buckets, n_chunks = NZ * NX * NC, rows_dev // 128
     below = (iota((128, 256), 0) <= iota((128, 256), 1)) | (iota((128, 256), 1) >= 128)
@@ -115,6 +192,9 @@
             jnp.sum(spot, axis=0, keepdims=True), (8, 128)
         )
 
+    smalls[1].wait()
+    smalls[2].wait()
+
     weights = jnp.broadcast_to(1.0 / sigma_ref[...], (128, 128)).T
     w_high, w_mid = split(weights)
     w_low = (weights - w_high.astype(F32) - w_mid.astype(F32)).astype(BF16)
@@ -153,7 +233,7 @@
             device_id={"rows": row_index(*offsets(g, j))}, device_id_type=MESH,
         )
 
-    def sort_and_send(g):
+    def sort(g):
         for j in range(per_group):
             first = row_index(*offsets(g, j)) * block
             for i in range(block // 8):
@@ -164,7 +244,9 @@
         part = pl.ds(pl.multiple_of(g * chunk, chunk), chunk)
         pick = pick_ref[...]
         sorted_ref[part, :] = dot(pick, high_ref[...]) + dot(pick, low_ref[...])
-        for j in range(per_group):
+
+    def send(g, first=0, last=NZ):
+        for j in range(first, last):
             if STEPS[j] == 0:
                 own = is_own(g, j)
                 spot = pl.ds(pl.multiple_of(g * chunk + j * block, block), block)
@@ -179,12 +261,18 @@
             else:
                 row_copy(g, j).start()
 
-    def sort_groups(first, last):
-        @pl.loop(first, last)
+    def sort_group(which):
+        @pl.loop(which, which + 1)
         def _(g):
-            sort_and_send(g)
-
-    sort_groups(0, 1)
+            sort(g)
+
+    def send_group(which, first=0, last=NZ):
+        @pl.loop(which, which + 1)
+        def _(g):
+            send(g, first, last)
+
+    sort_group(0)
+    send_group(0)
 
     gram_ref[...] = jnp.zeros_like(gram_ref)
 
@@ -205,9 +293,10 @@
     )
     pair.start()
 
+    smalls[3].wait()
     prior = prior_ref[...]
     prior_gram_ref[...] = exact_dot(prior, prior, ((0,), (0,)))
-    sort_groups(1, 2)
+    sort_group(1)
     pair.wait_recv()
     half_ref[...] = gram_ref[mine_half, :] + pair_ref[...]
 
@@ -224,7 +313,8 @@
         )
         copy.start()
         plane_copies.append(copy)
-    sort_groups(2, 4)
+    send_group(1, 0, 4)
+    sort_group(2)
     for copy in plane_copies:
         copy.wait_recv()
     total = half_ref[piece(x, y), :]
@@ -240,7 +330,8 @@
         )
         copy.start()
         line_copies.append(copy)
-    sort_groups(4, 6)
+    send_group(1, 4, 8)
+    sort_group(3)
     for copy in line_copies:
         copy.wait_recv()
     done = tiles_ref[z]
@@ -255,7 +346,8 @@
         )
         copy.start()
         back_copies.append(copy)
-    sort_groups(6, 8)
+    send_group(2, 0, 4)
+    sort_group(4)
     for copy in back_copies:
         copy.wait_recv()
     own_piece = pl.ds(
@@ -272,6 +364,8 @@
         )
         copy.start()
         plane_back.append(copy)
+    send_group(2, 4, 8)
+    sort_group(5)
     for copy in plane_back:
         copy.wait_recv()
     pair_back = pltpu.make_async_remote_copy(
@@ -279,30 +373,23 @@
         device_id=partner, device_id_type=MESH,
     )
     pair_back.start()
+    send_group(3, 0, 4)
+    sort_group(6)
     for copies in ([pair], plane_copies, line_copies, back_copies, plane_back):
         for copy in copies:
             copy.wait_send()
     pair_back.wait()
+    send_group(3, 4, 8)
+
+    @pl.loop(4, 7)
+    def _(g):
+        send(g)
+
+    sort_group(7)
+    send_group(7)
 
     gram_ref[...] = prior_gram_ref[...] + info_ref[...] / jnp.float32(total_rows)
-    inv_ref[...] = jnp.where(iota((state, state), 0) == iota((state, state), 1), jnp.float32(1.0), jnp.float32(0.0))
-
-    @pl.loop(0, state // PANEL)
-    def _(k):
-        part = pl.ds(pl.multiple_of(k * PANEL, PANEL), PANEL)
-        upper, inverse = factor_panel(gram_ref[part, part])
-        del upper
-        wide = exact_dot(inverse, gram_ref[part, :])
-        wide_inv = exact_dot(inverse, inv_ref[part, :])
-        row_no = k * PANEL + iota((PANEL, state), 0)
-        col_no = iota((PANEL, state), 1)
-        wide = jnp.where(col_no >= row_no, wide, jnp.float32(0.0))
-        factor_ref[part, :] = wide
-        inv_ref[part, :] = wide_inv
-        rest = jnp.where(col_no >= (k + 1) * PANEL, wide, jnp.float32(0.0))
-        gram_ref[...] = gram_ref[...] - exact_dot(rest, wide, ((0,), (0,)))
-        inv_ref[...] = inv_ref[...] - exact_dot(rest, wide_inv, ((0,), (0,)))
-
+    factor_and_invert(gram_ref, factor_ref, inv_ref)
     inv_high_ref[...], inv_low_ref[...] = split(inv_ref[...])
 
     @pl.loop(0, groups)
@@ -326,6 +413,17 @@
             out_ref[spot, :] = white[j * block : (j + 1) * block]
 
 
+def copy_out(white_ref, factor_ref, white_out, factor_out, sem):
+    copies = [
+        pltpu.make_async_copy(white_ref, white_out, sem.at[0]),
+        pltpu.make_async_copy(factor_ref, factor_out, sem.at[1]),
+    ]
+    for copy in copies:
+        copy.start()
+    for copy in copies:
+        copy.wait()
+
+
 def shards(observations, sensor_ids, sensor_sigma, buckets, prior_factor):
     rows_dev, state = observations.shape
     total_rows = rows_dev * lax.axis_size(("rows", "grp"))
@@ -333,15 +431,16 @@
     half = state // NC
     piece = half // (NX * NY)
     dma = pltpu.SemaphoreType.DMA
-    return pl.pallas_call(
+    whitened, factor = pl.pallas_call(
         functools.partial(kernel, total_rows),
-        out_shape=(
-            jax.ShapeDtypeStruct((rows_dev, state), F32),
-            jax.ShapeDtypeStruct((state, state), F32),
-        ),
-        in_specs=[pl.BlockSpec(memory_space=pl.ANY), vmem, vmem, vmem, vmem],
+        out_shape=(pltpu.VMEM((rows_dev, state), F32), pltpu.VMEM((state, state), F32)),
+        in_specs=[pl.BlockSpec(memory_space=pltpu.HBM)] * 5,
         out_specs=(vmem, vmem),
         scratch_shapes=[
+            pltpu.VMEM((rows_dev // 128, 128), I32),
+            pltpu.VMEM((1, sensor_sigma.shape[0]), F32),
+            pltpu.VMEM((rows_dev // 128, 128), I32),
+            pltpu.VMEM((state, state), F32),
             pltpu.VMEM((rows_dev, state), F32),
             pltpu.VMEM((rows_dev, state), BF16),
             pltpu.VMEM((rows_dev, state), BF16),
@@ -362,6 +461,7 @@
             pltpu.VMEM((state, state), F32),
             pltpu.VMEM((state, state), BF16),
             pltpu.VMEM((state, state), BF16),
+            dma((4,)),
             dma((NX * NC,)),
             dma((NZ * NX * NC,)),
             dma((NZ * NX * NC,)),
@@ -373,15 +473,31 @@
             dma((2,)),
         ],
         compiler_params=pltpu.CompilerParams(
-            collective_id=0, has_side_effects=True, vmem_limit_bytes=48 << 20
+            collective_id=0, has_side_effects=True, vmem_limit_bytes=34 << 20
         ),
     )(
-        observations,
-        sensor_ids.reshape(-1, 128),
-        sensor_sigma.reshape(1, -1),
-        buckets.reshape(-1, 128),
-        prior_factor,
+        *(
+            pltpu.with_memory_space_constraint(array, pltpu.HBM)
+            for array in (
+                observations,
+                sensor_ids.reshape(-1, 128),
+                sensor_sigma.reshape(1, -1),
+                buckets.reshape(-1, 128),
+                prior_factor,
+            )
+        )
     )
+    return pl.pallas_call(
+        copy_out,
+        out_shape=(
+            jax.ShapeDtypeStruct((rows_dev, state), F32),
+            jax.ShapeDtypeStruct((state, state), F32),
+        ),
+        in_specs=[pl.BlockSpec(memory_space=pl.ANY)] * 2,
+        out_specs=(pl.BlockSpec(memory_space=pl.ANY),) * 2,
+        scratch_shapes=[dma((2,))],
+        compiler_params=pltpu.CompilerParams(vmem_limit_bytes=1 << 20),
+    )(*(pltpu.with_memory_space_constraint(array, pltpu.VMEM) for array in (whitened, factor)))
 
 
 def solution(mesh):

time: 171 us -> 122 us (0.71)
  Pallas kernels: 161 us -> 121 us
  local copies, waits for them, and re-layouts: 8.88 us -> 0 us
    pallas_call x1 -> x2, Pallas kernels: 161 us -> 121 us  [the longest x1 119 us: shards(): pl.pallas_call(functools.partial(kernel, total_rows), out_shape=(pltpu.VM...]
    unnamed x10 -> x0, local copies, waits for them, and re-layouts: 8.88 us -> none
where the time goes in v2:
time: 122 us
  Pallas kernels  121 us (99%)
    pallas_call x1, Pallas kernels, shards(): pl.pallas_call(functools.partial(kernel, total_rows), out_shape=(pltpu.VM...  119 us

profile of v2, /device:TPU:1, one launch (start us, length us, event | category | flops | bytes accessed | tf_op | source)
XLA Modules:
  0.0 122.2 jit_solution(13224732664242736353)
XLA Ops:
  0.6 119.0 %shard_map.68 = (f32[2048,512]{1,0:T(8,128)S(1)}, f32[512,512]{1,0:T(8,128)S(1)}) custom-call(f32[2048,512]{1,0:T(8,128)} %x_hbm.1, s32[16,128]{1,0:T(8,128)} %bitcast.3, f32[1,128]{1,0:T(1,128)} %bitcast.5, s32[16,128]{1,0:T(8,128)} %bitcast.4, f32[512,512]{1,0:T(8,128)} %prior_hbm.1), custom_call_target="tpu_custom_call" | custom-call | tf_op jit(solution)/shard_map/pallas_call | solution.py:434
  119.7 2.4 %shard_map.69 = (f32[2048,512]{1,0:T(8,128)}, f32[512,512]{1,0:T(8,128)}) custom-call(f32[2048,512]{1,0:T(8,128)S(1)} %get-tuple-element.4.white_ref, f32[512,512]{1,0:T(8,128)S(1)} %get-tuple-element.5.factor_ref), custom_call_target="tpu_custom_call" | custom-call | tf_op jit(solution)/shard_map/pallas_call | solution.py:490

commit v3 on v2

--- a/solution.py
+++ b/solution.py
@@ -12,6 +12,7 @@
 NZ, NX, NC, NY = 8, 4, 2, 4
 STEPS = (4, 1, 7, 3, 5, 2, 6, 0)
 PANEL = 128
+PACE = 6
 
 
 def iota(shape, dim):
@@ -155,10 +156,12 @@
     ]
     for copy in smalls[:3]:
         copy.start()
-    for g in range(groups):
-        part = pl.ds(g * chunk, chunk)
-        copy = pltpu.make_async_copy(x_hbm.at[part], x_buf.at[part], x_sem.at[g])
-        copy.start()
+    def load(n):
+        part = pl.ds(pl.multiple_of(n * 2 * chunk, 2 * chunk), 2 * chunk)
+        return pltpu.make_async_copy(x_hbm.at[part], x_buf.at[part], x_sem.at[n])
+
+    for n in range(groups // 2):
+        load(n).start()
     smalls[3].start()
 
     barrier = pltpu.get_barrier_semaphore()
@@ -207,8 +210,11 @@
 
     @pl.loop(0, groups)
     def _(g):
+        @pl.when(g % 2 == 0)
+        def _():
+            load(g // 2).wait()
+
         part = pl.ds(pl.multiple_of(g * chunk, chunk), chunk)
-        pltpu.make_async_copy(x_hbm.at[part], x_buf.at[part], x_sem.at[g]).wait()
         scale = scale_ref[part, :]
         for n in range(state // 128):
             cols = slice(128 * n, 128 * n + 128)
@@ -226,23 +232,27 @@
         return (dz == 0) & (dx == 0) & (dc == 0)
 
     def row_copy(g, j):
-        spot = pl.ds(pl.multiple_of(g * chunk + j * block, block), block)
+        return blocks_copy(g, j, 1)
+
+    def blocks_copy(g, j, count):
+        spot = pl.ds(pl.multiple_of(g * chunk + j * block, block), count * block)
         return pltpu.make_async_remote_copy(
             sorted_ref.at[spot], recv_ref.at[spot],
-            send_sem.at[g * per_group + j], recv_sem.at[g * per_group + j],
+            send_sem.at[0], recv_sem.at[g],
             device_id={"rows": row_index(*offsets(g, j))}, device_id_type=MESH,
         )
 
-    def sort(g):
-        for j in range(per_group):
+    def sort(g, start=0, stop=NZ):
+        for j in range(start, stop):
             first = row_index(*offsets(g, j)) * block
             for i in range(block // 8):
                 hit = target_ref[...] == iota((8, rows_dev), 0) + (first + 8 * i)
                 pick_ref[j * block + 8 * i : j * block + 8 * i + 8, :] = jnp.where(
                     hit, jnp.float32(1.0), jnp.float32(0.0)
                 ).astype(BF16)
-        part = pl.ds(pl.multiple_of(g * chunk, chunk), chunk)
-        pick = pick_ref[...]
+        size = (stop - start) * block
+        part = pl.ds(pl.multiple_of(g * chunk + start * block, block), size)
+        pick = pick_ref[start * block : stop * block, :]
         sorted_ref[part, :] = dot(pick, high_ref[...]) + dot(pick, low_ref[...])
 
     def send(g, first=0, last=NZ):
@@ -261,18 +271,31 @@
             else:
                 row_copy(g, j).start()
 
-    def sort_group(which):
+    def sort_group(which, start=0, stop=NZ):
         @pl.loop(which, which + 1)
         def _(g):
-            sort(g)
-
-    def send_group(which, first=0, last=NZ):
-        @pl.loop(which, which + 1)
-        def _(g):
-            send(g, first, last)
-
-    sort_group(0)
-    send_group(0)
+            sort(g, start, stop)
+
+    def send_slots(first, last):
+        while first < last:
+            which, start = first // per_group, first % per_group
+            stop = min(per_group, start + last - first)
+
+            @pl.loop(which, which + 1)
+            def _(g):
+                send(g, start, stop)
+
+            first += stop - start
+
+    def send_next(count):
+        send_slots(sent[0], sent[0] + count)
+        sent[0] += count
+
+    sent = [0]
+    sort_group(0, 0, NZ // 2)
+    send_next(NZ // 2)
+    sort_group(0, NZ // 2, NZ)
+    send_next(NZ // 2)
 
     gram_ref[...] = jnp.zeros_like(gram_ref)
 
@@ -297,96 +320,97 @@
     prior = prior_ref[...]
     prior_gram_ref[...] = exact_dot(prior, prior, ((0,), (0,)))
     sort_group(1)
+    send_next(PACE)
+    sort_group(2)
     pair.wait_recv()
     half_ref[...] = gram_ref[mine_half, :] + pair_ref[...]
 
     def piece(px, py):
         return pl.ds(pl.multiple_of((px * NY + py) * piece_rows, piece_rows), piece_rows)
 
+    others = NX * NY - 1
+
+    def whole(source, target, sems):
+        return pltpu.make_async_remote_copy(
+            source, target, sems.at[0], sems.at[1], device_id=partner, device_id_type=MESH
+        )
+
     plane = [(dx, dy) for dx in range(NX) for dy in range(NY) if (dx, dy) != (0, 0)]
-    plane_copies = []
     for n, (dx, dy) in enumerate(plane):
         px, py = (x + dx) % NX, (y + dy) % NY
         copy = pltpu.make_async_remote_copy(
-            half_ref.at[piece(px, py)], plane_ref.at[n], plane_sem.at[0, n], plane_sem.at[1, n],
+            half_ref.at[piece(px, py)], plane_ref.at[n], plane_sem.at[0], plane_sem.at[1],
             device_id={"rows": row_index(0, dx, 0), "grp": py}, device_id_type=MESH,
         )
         copy.start()
-        plane_copies.append(copy)
-    send_group(1, 0, 4)
-    sort_group(2)
-    for copy in plane_copies:
-        copy.wait_recv()
+    send_next(PACE)
+    sort_group(3)
+    plane_all = whole(half_ref.at[pl.ds(0, others * piece_rows)], plane_ref, plane_sem)
+    plane_all.wait_recv()
     total = half_ref[piece(x, y), :]
     for n in range(len(plane)):
         total = total + plane_ref[n]
     for t in range(NZ):
         tiles_ref[t] = total[8 * (t // 4) : 8 * (t // 4) + 8, 128 * (t % 4) : 128 * (t % 4) + 128]
-    line_copies = []
     for dz in range(1, NZ):
         copy = pltpu.make_async_remote_copy(
-            tiles_ref.at[(z + dz) % NZ], line_ref.at[dz], line_sem.at[0, dz], line_sem.at[1, dz],
+            tiles_ref.at[(z + dz) % NZ], line_ref.at[dz - 1], line_sem.at[0], line_sem.at[1],
             device_id={"rows": row_index(dz, 0, 0)}, device_id_type=MESH,
         )
         copy.start()
-        line_copies.append(copy)
-    send_group(1, 4, 8)
-    sort_group(3)
-    for copy in line_copies:
-        copy.wait_recv()
+    send_next(PACE)
+    sort_group(4)
+    line_all = whole(tiles_ref.at[pl.ds(0, NZ - 1)], line_ref, line_sem)
+    line_all.wait_recv()
     done = tiles_ref[z]
     for dz in range(1, NZ):
-        done = done + line_ref[dz]
+        done = done + line_ref[dz - 1]
     gather_ref[z] = done
-    back_copies = []
     for dz in range(1, NZ):
         copy = pltpu.make_async_remote_copy(
-            gather_ref.at[z], gather_ref.at[z], line_back_sem.at[0, dz], line_back_sem.at[1, dz],
+            gather_ref.at[z], gather_ref.at[z], line_back_sem.at[0], line_back_sem.at[1],
             device_id={"rows": row_index(dz, 0, 0)}, device_id_type=MESH,
         )
         copy.start()
-        back_copies.append(copy)
-    send_group(2, 0, 4)
-    sort_group(4)
-    for copy in back_copies:
-        copy.wait_recv()
+    send_next(PACE)
+    sort_group(5)
+    back_tiles = gather_ref.at[pl.ds(0, NZ - 1)]
+    back_all = whole(back_tiles, back_tiles, line_back_sem)
+    back_all.wait_recv()
     own_piece = pl.ds(
         pl.multiple_of(c * half_rows + (x * NY + y) * piece_rows, piece_rows), piece_rows
     )
     info_ref[own_piece, :] = jnp.concatenate(
         [jnp.concatenate([gather_ref[4 * a + b] for b in range(4)], axis=1) for a in range(2)], axis=0
     )
-    plane_back = []
     for n, (dx, dy) in enumerate(plane):
         copy = pltpu.make_async_remote_copy(
-            info_ref.at[own_piece], info_ref.at[own_piece], plane_back_sem.at[0, n], plane_back_sem.at[1, n],
+            info_ref.at[own_piece], info_ref.at[own_piece], plane_back_sem.at[0], plane_back_sem.at[1],
             device_id={"rows": row_index(0, dx, 0), "grp": (y + dy) % NY}, device_id_type=MESH,
         )
         copy.start()
-        plane_back.append(copy)
-    send_group(2, 4, 8)
-    sort_group(5)
-    for copy in plane_back:
-        copy.wait_recv()
+    send_next(PACE)
+    sort_group(6)
+    back_pieces = info_ref.at[pl.ds(0, others * piece_rows)]
+    plane_back_all = whole(back_pieces, back_pieces, plane_back_sem)
+    plane_back_all.wait_recv()
     pair_back = pltpu.make_async_remote_copy(
         info_ref.at[mine_half], info_ref.at[mine_half], pair_back_sem.at[0], pair_back_sem.at[1],
         device_id=partner, device_id_type=MESH,
     )
     pair_back.start()
-    send_group(3, 0, 4)
-    sort_group(6)
-    for copies in ([pair], plane_copies, line_copies, back_copies, plane_back):
-        for copy in copies:
-            copy.wait_send()
+    send_next(PACE)
+    sort_group(7)
+    for copy in (pair, plane_all, line_all, back_all, plane_back_all):
+        copy.wait_send()
     pair_back.wait()
-    send_group(3, 4, 8)
-
-    @pl.loop(4, 7)
+    send_next(-sent[0] % per_group)
+
+    @pl.loop(sent[0] // per_group, groups - 1)
     def _(g):
         send(g)
 
-    sort_group(7)
-    send_group(7)
+    send_slots((groups - 1) * per_group, groups * per_group)
 
     gram_ref[...] = prior_gram_ref[...] + info_ref[...] / jnp.float32(total_rows)
     factor_and_invert(gram_ref, factor_ref, inv_ref)
@@ -394,13 +418,16 @@
 
     @pl.loop(0, groups)
     def _(g):
-        for j in range(per_group):
-            if STEPS[j] == 0:
-                @pl.when(jnp.logical_not(is_own(g, j)))
-                def _():
-                    row_copy(g, j).wait()
-            else:
-                row_copy(g, j).wait()
+        own = is_own(g, per_group - 1)
+
+        @pl.when(own)
+        def _():
+            blocks_copy(g, 0, per_group - 1).wait_recv()
+
+        @pl.when(jnp.logical_not(own))
+        def _():
+            blocks_copy(g, 0, per_group).wait_recv()
+
         part = pl.ds(pl.multiple_of(g * chunk, chunk), chunk)
         high, low = split(recv_ref[part, :])
         inv_high, inv_low = inv_high_ref[...], inv_low_ref[...]
@@ -411,6 +438,8 @@
             source = row_index(NZ - dz, NX - dx, NC - dc)
             spot = pl.ds(pl.multiple_of(source * block, block), block)
             out_ref[spot, :] = white[j * block : (j + 1) * block]
+
+    blocks_copy(0, 0, groups * per_group - 1).wait_send()
 
 
 def copy_out(white_ref, factor_ref, white_out, factor_out, sem):
@@ -454,7 +483,7 @@
             pltpu.VMEM((half, state), F32),
             pltpu.VMEM((NX * NY - 1, piece, state), F32),
             pltpu.VMEM((NZ, 8, 128), F32),
-            pltpu.VMEM((NZ, 8, 128), F32),
+            pltpu.VMEM((NZ - 1, 8, 128), F32),
             pltpu.VMEM((NZ, 8, 128), F32),
             pltpu.VMEM((state, state), F32),
             pltpu.VMEM((state, state), F32),
@@ -462,14 +491,14 @@
             pltpu.VMEM((state, state), BF16),
             pltpu.VMEM((state, state), BF16),
             dma((4,)),
+            dma((NX * NC // 2,)),
+            dma((1,)),
             dma((NX * NC,)),
-            dma((NZ * NX * NC,)),
-            dma((NZ * NX * NC,)),
             dma((2,)),
-            dma((2, NX * NY - 1)),
-            dma((2, NZ)),
-            dma((2, NZ)),
-            dma((2, NX * NY - 1)),
+            dma((2,)),
+            dma((2,)),
+            dma((2,)),
+            dma((2,)),
             dma((2,)),
         ],
         compiler_params=pltpu.CompilerParams(

time: 122 us -> 114 us (0.934)
  Pallas kernels: 121 us -> 113 us
    pallas_call x1, Pallas kernels: 119 us -> 110 us  [shards(): pl.pallas_call(functools.partial(kernel, total_rows), out_shape=(pltpu.VM...]
where the time goes in v3:
time: 114 us
  Pallas kernels  113 us (99%)
    pallas_call x1, Pallas kernels, shards(): pl.pallas_call(functools.partial(kernel, total_rows), out_shape=(pltpu.VM...  110 us
    pallas_call x1, Pallas kernels, shards(): pl.pallas_call(copy_out, out_shape=(jax.ShapeDtypeStruct((rows_dev, state...  2.37 us

profile of v3, /device:TPU:1, one launch (start us, length us, event | category | flops | bytes accessed | tf_op | source)
XLA Modules:
  0.0 113.5 jit_solution(959035323347454789)
XLA Ops:
  0.6 110.4 %shard_map.68 = (f32[2048,512]{1,0:T(8,128)S(1)}, f32[512,512]{1,0:T(8,128)S(1)}) custom-call(f32[2048,512]{1,0:T(8,128)} %x_hbm.1, s32[16,128]{1,0:T(8,128)} %bitcast.3, f32[1,128]{1,0:T(1,128)} %bitcast.5, s32[16,128]{1,0:T(8,128)} %bitcast.4, f32[512,512]{1,0:T(8,128)} %prior_hbm.1), custom_call_target="tpu_custom_call" | custom-call | tf_op jit(solution)/shard_map/pallas_call | solution.py:463
  111.0 2.4 %shard_map.69 = (f32[2048,512]{1,0:T(8,128)}, f32[512,512]{1,0:T(8,128)}) custom-call(f32[2048,512]{1,0:T(8,128)S(1)} %get-tuple-element.4.white_ref, f32[512,512]{1,0:T(8,128)S(1)} %get-tuple-element.5.factor_ref), custom_call_target="tpu_custom_call" | custom-call | tf_op jit(solution)/shard_map/pallas_call | solution.py:519

commit v4 on v3

--- a/solution.py
+++ b/solution.py
@@ -148,22 +148,6 @@
     def row_index(dz, dx, dc):
         return (((z + dz) % NZ) * NX + (x + dx) % NX) * NC + (c + dc) % NC
 
-    smalls = [
-        pltpu.make_async_copy(source, target, small_sem.at[n])
-        for n, (source, target) in enumerate(
-            ((buckets_hbm, buckets_ref), (ids_hbm, ids_ref), (sigma_hbm, sigma_ref), (prior_hbm, prior_ref))
-        )
-    ]
-    for copy in smalls[:3]:
-        copy.start()
-    def load(n):
-        part = pl.ds(pl.multiple_of(n * 2 * chunk, 2 * chunk), 2 * chunk)
-        return pltpu.make_async_copy(x_hbm.at[part], x_buf.at[part], x_sem.at[n])
-
-    for n in range(groups // 2):
-        load(n).start()
-    smalls[3].start()
-
     barrier = pltpu.get_barrier_semaphore()
     for dz in range(NZ):
         for dx in range(NX):
@@ -176,6 +160,22 @@
         for dy in range(1, NY):
             peer = {"rows": row_index(0, dx, 0), "grp": (y + dy) % NY}
             pl.semaphore_signal(barrier, inc=1, device_id=peer, device_id_type=MESH)
+
+    smalls = [
+        pltpu.make_async_copy(source, target, small_sem.at[n])
+        for n, (source, target) in enumerate(
+            ((buckets_hbm, buckets_ref), (ids_hbm, ids_ref), (sigma_hbm, sigma_ref), (prior_hbm, prior_ref))
+        )
+    ]
+    for copy in smalls[:3]:
+        copy.start()
+    def load(n):
+        part = pl.ds(pl.multiple_of(n * 2 * chunk, 2 * chunk), 2 * chunk)
+        return pltpu.make_async_copy(x_hbm.at[part], x_buf.at[part], x_sem.at[n])
+
+    for n in range(groups // 2):
+        load(n).start()
+    smalls[3].start()
 
     smalls[0].wait()
 
@@ -222,8 +222,6 @@
             high_ref[part, cols] = high
             low_ref[part, cols] = low
 
-    pl.semaphore_wait(barrier, NZ * NX * NC - 1 + NX * (NY - 1))
-
     def offsets(g, j):
         return STEPS[j], (g // NC + j) % NX, g % NC
 
@@ -292,10 +290,9 @@
         sent[0] += count
 
     sent = [0]
-    sort_group(0, 0, NZ // 2)
-    send_next(NZ // 2)
-    sort_group(0, NZ // 2, NZ)
-    send_next(NZ // 2)
+    sort_group(0)
+    pl.semaphore_wait(barrier, NZ * NX * NC - 1 + NX * (NY - 1))
+    send_next(per_group)
 
     gram_ref[...] = jnp.zeros_like(gram_ref)
 
@@ -401,9 +398,8 @@
     pair_back.start()
     send_next(PACE)
     sort_group(7)
-    for copy in (pair, plane_all, line_all, back_all, plane_back_all):
-        copy.wait_send()
-    pair_back.wait()
+    pair.wait_send()
+    pair_back.wait_recv()
     send_next(-sent[0] % per_group)
 
     @pl.loop(sent[0] // per_group, groups - 1)
@@ -440,6 +436,8 @@
             out_ref[spot, :] = white[j * block : (j + 1) * block]
 
     blocks_copy(0, 0, groups * per_group - 1).wait_send()
+    for copy in (plane_all, line_all, back_all, plane_back_all, pair_back):
+        copy.wait_send()
 
 
 def copy_out(white_ref, factor_ref, white_out, factor_out, sem):

time: 114 us -> 110 us (0.965)
  Pallas kernels: 113 us -> 109 us
    pallas_call x1, Pallas kernels: 110 us -> 107 us  [shards(): pl.pallas_call(functools.partial(kernel, total_rows), out_shape=(pltpu.VM...]
where the time goes in v4:
time: 110 us
  Pallas kernels  109 us (99%)
    pallas_call x1, Pallas kernels, shards(): pl.pallas_call(functools.partial(kernel, total_rows), out_shape=(pltpu.VM...  107 us
    pallas_call x1, Pallas kernels, shards(): pl.pallas_call(copy_out, out_shape=(jax.ShapeDtypeStruct((rows_dev, state...  2.37 us

profile of v4, /device:TPU:1, one launch (start us, length us, event | category | flops | bytes accessed | tf_op | source)
XLA Modules:
  0.0 110.2 jit_solution(12817267359547459198)
XLA Ops:
  0.6 107.1 %shard_map.68 = (f32[2048,512]{1,0:T(8,128)S(1)}, f32[512,512]{1,0:T(8,128)S(1)}) custom-call(f32[2048,512]{1,0:T(8,128)} %x_hbm.1, s32[16,128]{1,0:T(8,128)} %bitcast.3, f32[1,128]{1,0:T(1,128)} %bitcast.5, s32[16,128]{1,0:T(8,128)} %bitcast.4, f32[512,512]{1,0:T(8,128)} %prior_hbm.1), custom_call_target="tpu_custom_call" | custom-call | tf_op jit(solution)/shard_map/pallas_call | solution.py:461
  107.7 2.4 %shard_map.69 = (f32[2048,512]{1,0:T(8,128)}, f32[512,512]{1,0:T(8,128)}) custom-call(f32[2048,512]{1,0:T(8,128)S(1)} %get-tuple-element.4.white_ref, f32[512,512]{1,0:T(8,128)S(1)} %get-tuple-element.5.factor_ref), custom_call_target="tpu_custom_call" | custom-call | tf_op jit(solution)/shard_map/pallas_call | solution.py:517

commit v5 on v4

--- a/solution.py
+++ b/solution.py
@@ -12,7 +12,7 @@
 NZ, NX, NC, NY = 8, 4, 2, 4
 STEPS = (4, 1, 7, 3, 5, 2, 6, 0)
 PANEL = 128
-PACE = 6
+PACE = 7
 
 
 def iota(shape, dim):
@@ -290,15 +290,17 @@
         sent[0] += count
 
     sent = [0]
-    sort_group(0)
+    sort_group(0, 0, per_group // 2)
     pl.semaphore_wait(barrier, NZ * NX * NC - 1 + NX * (NY - 1))
-    send_next(per_group)
+    send_next(per_group // 2)
+    sort_group(0, per_group // 2, per_group)
+    send_next(2)
 
     gram_ref[...] = jnp.zeros_like(gram_ref)
 
-    @pl.loop(0, groups)
+    @pl.loop(0, groups // 2)
     def _(g):
-        part = pl.ds(pl.multiple_of(g * chunk, chunk), chunk)
+        part = pl.ds(pl.multiple_of(g * 2 * chunk, 2 * chunk), 2 * chunk)
         high, low = high_ref[part, :], low_ref[part, :]
         along = ((0,), (0,))
         gram_ref[...] += dot(high, high, along) + dot(high, low, along) + dot(low, high, along)
@@ -312,6 +314,7 @@
         gram_ref.at[other_half], pair_ref, pair_sem.at[0], pair_sem.at[1], device_id=partner, device_id_type=MESH
     )
     pair.start()
+    send_next(per_group // 2 - 2)
 
     smalls[3].wait()
     prior = prior_ref[...]

time: 110 us -> 110 us (level)
  no operation moved by 1% of the time
where the time goes in v5:
time: 110 us
  Pallas kernels  109 us (99%)
    pallas_call x1, Pallas kernels, shards(): pl.pallas_call(functools.partial(kernel, total_rows), out_shape=(pltpu.VM...  107 us
    pallas_call x1, Pallas kernels, shards(): pl.pallas_call(copy_out, out_shape=(jax.ShapeDtypeStruct((rows_dev, state...  2.37 us

profile of v5, /device:TPU:1, one launch (start us, length us, event | category | flops | bytes accessed | tf_op | source)
XLA Modules:
  0.0 109.7 jit_solution(6310380724570563510)
XLA Ops:
  0.6 106.5 %shard_map.68 = (f32[2048,512]{1,0:T(8,128)S(1)}, f32[512,512]{1,0:T(8,128)S(1)}) custom-call(f32[2048,512]{1,0:T(8,128)} %x_hbm.1, s32[16,128]{1,0:T(8,128)} %bitcast.3, f32[1,128]{1,0:T(1,128)} %bitcast.5, s32[16,128]{1,0:T(8,128)} %bitcast.4, f32[512,512]{1,0:T(8,128)} %prior_hbm.1), custom_call_target="tpu_custom_call" | custom-call | tf_op jit(solution)/shard_map/pallas_call | solution.py:464
  107.2 2.4 %shard_map.69 = (f32[2048,512]{1,0:T(8,128)}, f32[512,512]{1,0:T(8,128)}) custom-call(f32[2048,512]{1,0:T(8,128)S(1)} %get-tuple-element.4.white_ref, f32[512,512]{1,0:T(8,128)S(1)} %get-tuple-element.5.factor_ref), custom_call_target="tpu_custom_call" | custom-call | tf_op jit(solution)/shard_map/pallas_call | solution.py:520

commit v6 on v5

--- a/solution.py
+++ b/solution.py
@@ -236,7 +236,7 @@
         spot = pl.ds(pl.multiple_of(g * chunk + j * block, block), count * block)
         return pltpu.make_async_remote_copy(
             sorted_ref.at[spot], recv_ref.at[spot],
-            send_sem.at[0], recv_sem.at[g],
+            send_sem.at[0], recv_sem.at[g * 2 + j // (per_group // 2)],
             device_id={"rows": row_index(*offsets(g, j))}, device_id_type=MESH,
         )
 
@@ -417,26 +417,30 @@
 
     @pl.loop(0, groups)
     def _(g):
-        own = is_own(g, per_group - 1)
-
-        @pl.when(own)
-        def _():
-            blocks_copy(g, 0, per_group - 1).wait_recv()
-
-        @pl.when(jnp.logical_not(own))
-        def _():
-            blocks_copy(g, 0, per_group).wait_recv()
-
-        part = pl.ds(pl.multiple_of(g * chunk, chunk), chunk)
-        high, low = split(recv_ref[part, :])
-        inv_high, inv_low = inv_high_ref[...], inv_low_ref[...]
-        cross = ((1,), (1,))
-        white = dot(high, inv_high, cross) + dot(high, inv_low, cross) + dot(low, inv_high, cross)
-        for j in range(per_group):
-            dz, dx, dc = offsets(g, j)
-            source = row_index(NZ - dz, NX - dx, NC - dc)
-            spot = pl.ds(pl.multiple_of(source * block, block), block)
-            out_ref[spot, :] = white[j * block : (j + 1) * block]
+        for start in (0, per_group // 2):
+            count = per_group // 2
+            if start:
+                own = is_own(g, per_group - 1)
+
+                @pl.when(own)
+                def _():
+                    blocks_copy(g, start, count - 1).wait_recv()
+
+                @pl.when(jnp.logical_not(own))
+                def _():
+                    blocks_copy(g, start, count).wait_recv()
+            else:
+                blocks_copy(g, start, count).wait_recv()
+            part = pl.ds(pl.multiple_of(g * chunk + start * block, block), count * block)
+            high, low = split(recv_ref[part, :])
+            inv_high, inv_low = inv_high_ref[...], inv_low_ref[...]
+            cross = ((1,), (1,))
+            white = dot(high, inv_high, cross) + dot(high, inv_low, cross) + dot(low, inv_high, cross)
+            for j in range(count):
+                dz, dx, dc = offsets(g, start + j)
+                source = row_index(NZ - dz, NX - dx, NC - dc)
+                spot = pl.ds(pl.multiple_of(source * block, block), block)
+                out_ref[spot, :] = white[j * block : (j + 1) * block]
 
     blocks_copy(0, 0, groups * per_group - 1).wait_send()
     for copy in (plane_all, line_all, back_all, plane_back_all, pair_back):
@@ -494,7 +498,7 @@
             dma((4,)),
             dma((NX * NC // 2,)),
             dma((1,)),
-            dma((NX * NC,)),
+            dma((2 * NX * NC,)),
             dma((2,)),
             dma((2,)),
             dma((2,)),

time: 110 us -> 115 us (1.045)
  Pallas kernels: 109 us -> 114 us
    pallas_call x1, Pallas kernels: 107 us -> 112 us  [shards(): pl.pallas_call(functools.partial(kernel, total_rows), out_shape=(pltpu.VM...]
where the time goes in v6:
time: 115 us
  Pallas kernels  114 us (99%)
    pallas_call x1, Pallas kernels, shards(): pl.pallas_call(functools.partial(kernel, total_rows), out_shape=(pltpu.VM...  112 us
    pallas_call x1, Pallas kernels, shards(): pl.pallas_call(copy_out, out_shape=(jax.ShapeDtypeStruct((rows_dev, state...  2.37 us

profile of v6, /device:TPU:1, one launch (start us, length us, event | category | flops | bytes accessed | tf_op | source)
XLA Modules:
  0.0 115.2 jit_solution(16389352400932912624)
XLA Ops:
  0.6 112.1 %shard_map.68 = (f32[2048,512]{1,0:T(8,128)S(1)}, f32[512,512]{1,0:T(8,128)S(1)}) custom-call(f32[2048,512]{1,0:T(8,128)} %x_hbm.1, s32[16,128]{1,0:T(8,128)} %bitcast.3, f32[1,128]{1,0:T(1,128)} %bitcast.5, s32[16,128]{1,0:T(8,128)} %bitcast.4, f32[512,512]{1,0:T(8,128)} %prior_hbm.1), custom_call_target="tpu_custom_call" | custom-call | tf_op jit(solution)/shard_map/pallas_call | solution.py:468
  112.7 2.4 %shard_map.69 = (f32[2048,512]{1,0:T(8,128)}, f32[512,512]{1,0:T(8,128)}) custom-call(f32[2048,512]{1,0:T(8,128)S(1)} %get-tuple-element.4.white_ref, f32[512,512]{1,0:T(8,128)S(1)} %get-tuple-element.5.factor_ref), custom_call_target="tpu_custom_call" | custom-call | tf_op jit(solution)/shard_map/pallas_call | solution.py:524
